TPU v7x, 32 devices: a whole 2x2x4 slice. The times are simulated.
32 devices in a mesh: section: 16 (over z, y, core), ctx: 2 (over x).
Axes of the slice: x: 2, y: 2, z: 4, core: 2. Of those that a mesh axis runs over, the one named last changes fastest.
Arguments:
- queries: bfloat16 [16, 256, 8192], P('section', 'ctx'), may hold values from -6 to 6
- key_states: bfloat16 [16, 256, 1024], P('section', 'ctx'), may hold values from -6 to 6
- value_states: bfloat16 [16, 256, 1024], P('section', 'ctx'), may hold values from -1.5 to 1.5
- out_grad: bfloat16 [16, 256, 8192], P('section', 'ctx'), may hold values from -6 to 6
- node_end: int32 [16, 256], P('section'), may hold values from 1 to 256, as said below
- block_list: int32 [16, 2, 2], P('section'), may hold values from 0 to 1, as said below
- block_count: int32 [16, 2], P('section'), may hold values from 1 to 2, as said below
Outputs:
- query_grads: bfloat16 [16, 256, 8192], P('section', 'ctx')
- key_grads: bfloat16 [16, 256, 1024], P('section', 'ctx')
- value_grads: bfloat16 [16, 256, 1024], P('section', 'ctx')
Inputs may be any that keep to these rules, and one draw needn't show every extreme that they name: Each section packs search trees one after another, each in preorder; node_end[s, j] is one past the last node of node j's subtree, so j is an ancestor of i (or i itself) exactly when j <= i < node_end[s, j]. Row b of block_list[s] lists, in increasing order, every key block that holds an ancestor (or the node itself) of some node of query block b, and no other; b itself is always listed; entries after the first block_count[s, b] are 0. block_count[s, b] is the number of listed key blocks of query block b, at most b + 1.
All inputs are finite; a program needn't handle non-finite values.
Results may differ from a plain program's by a relative error of at most 0.0053.
Values may be sent and summed in bfloat16 or wider, within the bound.
A program may use at most 128 MiB of HBM per device.

v0:
```python
import functools
import math

import jax
import jax.numpy as jnp
from jax import lax
from jax.experimental import pallas as pl
from jax.experimental.pallas import tpu as pltpu
from jax.sharding import PartitionSpec as P

HEADS = 64
KV_HEADS = 8
HEAD_DIM = 128
BLK = 128
RATIO = HEADS // KV_HEADS
PAIR = 2
WIDTH = RATIO * HEAD_DIM

F32 = jnp.float32
BF16 = jnp.bfloat16
MESH = pl.DeviceIdType.MESH


def contract(left, right, left_dim, right_dim):
    return lax.dot_general(
        left, right, (((left_dim,), (right_dim,)), ((), ())), preferred_element_type=F32
    )


def kernel(
    section_total,
    ctx_total,
    q_hbm,
    k_hbm,
    v_hbm,
    g_hbm,
    end_hbm,
    list_hbm,
    count_hbm,
    out_q,
    out_k,
    out_v,
    q_buf,
    g_buf,
    kv_buf,
    dq_buf,
    ds_buf,
    at_buf,
    bias,
    own,
    share,
    shares_in,
    final,
    end_ref,
    list_ref,
    count_ref,
    table_sem,
    load_sem,
    kv_sem,
    kv_send,
    kv_recv,
    dq_send,
    share_send,
    share_recv,
    final_send,
    out_recv,
):
    rows = q_hbm.shape[1]
    block_total = list_hbm.shape[1]
    blocks_here = rows // BLK
    scale = 1.0 / math.sqrt(HEAD_DIM)
    section = lax.axis_index("section")
    ctx = lax.axis_index("ctx")
    before = lax.rem(section + section_total - 1, section_total)
    after = lax.rem(section + 1, section_total)

    def cols(index, width=HEAD_DIM):
        return pl.ds(pl.multiple_of(index * width, width), width)

    def block(index):
        return pl.ds(pl.multiple_of(index * rows, rows), rows)

    barrier = pltpu.get_barrier_semaphore()
    for target in (before, after):
        pl.semaphore_signal(barrier, 1, device_id={"section": target}, device_id_type=MESH)
    for step in range(1, ctx_total):
        other = lax.rem(ctx + step, ctx_total)
        pl.semaphore_signal(barrier, 1, device_id={"ctx": other}, device_id_type=MESH)

    def load(group):
        for which, source in enumerate((k_hbm, v_hbm)):
            pltpu.make_async_copy(
                source.at[0, :, cols(group)], kv_buf.at[group, which, block(ctx)], kv_sem.at[group]
            ).start()
        for which, (source, target) in enumerate(((q_hbm, q_buf), (g_hbm, g_buf))):
            pltpu.make_async_copy(
                source.at[0, :, cols(group, WIDTH)], target.at[group], load_sem.at[which, group]
            ).start()

    tables = [
        pltpu.make_async_copy(source, target, table_sem.at[slot])
        for slot, (source, target) in enumerate(
            ((end_hbm, end_ref), (list_hbm, list_ref), (count_hbm, count_ref))
        )
    ]
    for table in tables:
        table.start()
    load(0)

    def kv_copy(group, which, source, peer):
        return pltpu.make_async_remote_copy(
            src_ref=(k_hbm, v_hbm)[which].at[0, :, cols(group)],
            dst_ref=kv_buf.at[group, which, block(source)],
            send_sem=kv_send.at[peer, group, which],
            recv_sem=kv_recv.at[source, group],
            device_id={"ctx": peer},
            device_id_type=MESH,
        )

    def share_copy(group, source, peer):
        return pltpu.make_async_remote_copy(
            src_ref=share.at[group, :, pl.ds(peer * rows, rows)],
            dst_ref=shares_in.at[group, source],
            send_sem=share_send.at[peer, group],
            recv_sem=share_recv.at[source, group],
            device_id={"ctx": peer},
            device_id_type=MESH,
        )

    def query_copy(group, pair):
        return pltpu.make_async_remote_copy(
            src_ref=dq_buf.at[group, :, cols(pair, PAIR * HEAD_DIM)],
            dst_ref=out_q.at[0, :, cols(group * (RATIO // PAIR) + pair, PAIR * HEAD_DIM)],
            send_sem=dq_send.at[group],
            recv_sem=out_recv.at[0],
            device_id={"section": before},
            device_id_type=MESH,
        )

    def final_copy(group, which):
        return pltpu.make_async_remote_copy(
            src_ref=final.at[group, which],
            dst_ref=(out_k, out_v)[which].at[0, :, cols(group)],
            send_sem=final_send.at[which, group],
            recv_sem=out_recv.at[1 + which],
            device_id={"section": before},
            device_id_type=MESH,
        )

    def fill_bias(key_blocks):
        for low in range(blocks_here):
            query_block = ctx * blocks_here + low
            position = query_block * BLK + lax.broadcasted_iota(jnp.int32, (BLK, BLK), 0)
            for key_block in range(key_blocks):
                listed = jnp.int32(0)
                for entry in range(block_total):
                    hit = (list_ref[0, query_block, entry] == key_block) & (
                        entry < count_ref[0, query_block]
                    )
                    listed = listed | hit.astype(jnp.int32)
                key_place = key_block * BLK + lax.broadcasted_iota(jnp.int32, (BLK, BLK), 1)
                end = end_ref[:, key_block * BLK : (key_block + 1) * BLK] * listed
                allowed = (key_place <= position) & (position < end)
                bias[
                    key_block * BLK : (key_block + 1) * BLK, low * BLK : (low + 1) * BLK
                ] = jnp.where(allowed, 0.0, -jnp.inf).astype(F32).T

    def run(mine):
        length = (mine + 1) * rows
        for table in tables:
            table.wait()
        fill_bias((mine + 1) * blocks_here)
        pl.loop(1, KV_HEADS)(load)

        def send_keys(group):
            for peer in range(mine + 1, ctx_total):
                for which in range(2):
                    kv_copy(group, which, mine, peer).start()

        def enter():
            pl.semaphore_wait(barrier, 1 + ctx_total)
            if mine < ctx_total - 1:
                pl.when(section % 2 == 0)(lambda: send_keys(0))

        late = mine == ctx_total - 1
        if not late:
            enter()
        span = PAIR * rows

        def per_group(group, carry):
            if mine < ctx_total - 1:
                pl.when((section % 2 == 0) & (group + 1 < KV_HEADS))(lambda: send_keys(group + 1))
                pl.when(section % 2 == 1)(lambda: send_keys(group))
            for source in range(mine):
                pltpu.make_async_copy(
                    kv_buf.at[group, :, pl.ds(source * rows, rows)],
                    kv_buf.at[group, :, pl.ds(source * rows, rows)],
                    kv_recv.at[source, group],
                ).wait()
            pltpu.make_async_copy(
                kv_buf.at[group, :, pl.ds(mine * rows, rows)],
                kv_buf.at[group, :, pl.ds(mine * rows, rows)],
                kv_sem.at[group],
            ).wait()
            pltpu.make_async_copy(q_buf.at[group], q_buf.at[group], load_sem.at[0, group]).wait()
            pltpu.make_async_copy(g_buf.at[group], g_buf.at[group], load_sem.at[1, group]).wait()
            keys = kv_buf[group, 0, 0:length, :]
            values = kv_buf[group, 1, 0:length, :]

            def stacked(ref, first, count):
                parts = [ref[group, :, cols(first + low)] for low in range(count)]
                return jnp.concatenate(parts, axis=0)

            def per_pair(pair):
                here = pl.ds(pl.multiple_of(pair * span, span), span)
                scores = contract(keys, stacked(q_buf, pair * PAIR, PAIR), 1, 1) * scale
                masked = bias[0:length, :]
                scores = scores + jnp.concatenate([masked] * PAIR, axis=1)
                exponent = jnp.exp(scores - jnp.max(scores, axis=0, keepdims=True))
                total = jnp.sum(exponent, axis=0, keepdims=True)
                attention = exponent * (1.0 / total)
                at_buf[0:length, here] = attention.astype(BF16)
                weight_grad = contract(values, stacked(g_buf, pair * PAIR, PAIR), 1, 1)
                row_delta = jnp.sum(attention * weight_grad, axis=0, keepdims=True)
                score_grad = (attention * (weight_grad - row_delta) * scale).astype(BF16)
                ds_buf[0:length, here] = score_grad
                query_grad = contract(score_grad, keys, 0, 0).astype(BF16)
                for low in range(PAIR):
                    dq_buf[group, :, cols(pair * PAIR + low)] = query_grad[low * rows : (low + 1) * rows]
                if late:
                    pl.when((group == 0) & (pair == 0))(enter)
                query_copy(group, pair).start()

            pl.loop(0, RATIO // PAIR)(per_pair)
            key_grad = contract(ds_buf[0:length, :], stacked(q_buf, 0, RATIO), 1, 0)
            value_grad = contract(at_buf[0:length, :], stacked(g_buf, 0, RATIO), 1, 0)
            first = mine * rows
            if mine > 0:
                share[group, 0, 0:first, :] = key_grad[0:first].astype(BF16)
                share[group, 1, 0:first, :] = value_grad[0:first].astype(BF16)
                for peer in range(mine):
                    share_copy(group, mine, peer).start()
            if mine == ctx_total - 1:
                final[group, 0] = key_grad[first:].astype(BF16)
                final[group, 1] = value_grad[first:].astype(BF16)
                for which in range(2):
                    final_copy(group, which).start()
            else:
                own[group, 0] = key_grad[first:]
                own[group, 1] = value_grad[first:]
            return carry

        lax.fori_loop(0, KV_HEADS, per_group, 0)

        if mine < ctx_total - 1:

            @pl.loop(0, KV_HEADS)
            def _(group):
                total = own[group]
                for source in range(mine + 1, ctx_total):
                    share_copy(group, source, mine).wait_recv()
                    total = total + shares_in[group, source].astype(F32)
                final[group] = total.astype(BF16)
                for which in range(2):
                    final_copy(group, which).start()

        @pl.loop(0, KV_HEADS)
        def _(group):
            for peer in range(mine + 1, ctx_total):
                for which in range(2):
                    kv_copy(group, which, mine, peer).wait_send()
            for peer in range(mine):
                share_copy(group, mine, peer).wait_send()

    for mine in range(ctx_total):
        pl.when(ctx == mine)(functools.partial(run, mine))

    @pl.loop(0, KV_HEADS)
    def _(group):
        pltpu.make_async_copy(dq_buf.at[group], dq_buf.at[group], dq_send.at[group]).wait()
        for which in range(2):
            final_copy(group, which).wait_send()

    for slot, out in enumerate((out_q, out_k, out_v)):
        pltpu.make_async_copy(out, out, out_recv.at[slot]).wait()


def write_out(held_q, held_k, held_v, out_q, out_k, out_v, done):
    pairs = ((held_q, out_q), (held_k, out_k), (held_v, out_v))
    copies = [pltpu.make_async_copy(a, b, done.at[slot]) for slot, (a, b) in enumerate(pairs)]
    for copy in copies:
        copy.start()
    for copy in copies:
        copy.wait()


def per_device(
    section_total,
    ctx_total,
    queries,
    key_states,
    value_states,
    out_grad,
    node_end,
    block_list,
    block_count,
):
    rows = queries.shape[1]
    length = node_end.shape[1]
    anywhere = pl.BlockSpec(memory_space=pl.ANY)
    vector = pl.BlockSpec(memory_space=pltpu.VMEM)
    dma = pltpu.SemaphoreType.DMA
    tall = RATIO * rows
    held = pl.pallas_call(
        functools.partial(kernel, section_total, ctx_total),
        out_shape=(
            pltpu.VMEM(queries.shape, BF16),
            pltpu.VMEM(key_states.shape, BF16),
            pltpu.VMEM(value_states.shape, BF16),
        ),
        in_specs=[anywhere] * 7,
        out_specs=[vector] * 3,
        scratch_shapes=[
            pltpu.VMEM((KV_HEADS, rows, WIDTH), BF16),
            pltpu.VMEM((KV_HEADS, rows, WIDTH), BF16),
            pltpu.VMEM((KV_HEADS, 2, length, HEAD_DIM), BF16),
            pltpu.VMEM((KV_HEADS, rows, WIDTH), BF16),
            pltpu.VMEM((length, tall), BF16),
            pltpu.VMEM((length, tall), BF16),
            pltpu.VMEM((length, rows), F32),
            pltpu.VMEM((KV_HEADS, 2, rows, HEAD_DIM), F32),
            pltpu.VMEM((KV_HEADS, 2, length, HEAD_DIM), BF16),
            pltpu.VMEM((KV_HEADS, ctx_total, 2, rows, HEAD_DIM), BF16),
            pltpu.VMEM((KV_HEADS, 2, rows, HEAD_DIM), BF16),
            pltpu.VMEM(node_end.shape, jnp.int32),
            pltpu.SMEM(block_list.shape, jnp.int32),
            pltpu.SMEM(block_count.shape, jnp.int32),
            dma((3,)),
            dma((2, KV_HEADS)),
            dma((KV_HEADS,)),
            dma((ctx_total, KV_HEADS, 2)),
            dma((ctx_total, KV_HEADS)),
            dma((KV_HEADS,)),
            dma((ctx_total, KV_HEADS)),
            dma((ctx_total, KV_HEADS)),
            dma((2, KV_HEADS)),
            dma((3,)),
        ],
        compiler_params=pltpu.CompilerParams(collective_id=0, has_side_effects=True),
    )(queries, key_states, value_states, out_grad, node_end, block_list, block_count)
    return pl.pallas_call(
        write_out,
        out_shape=tuple(jax.ShapeDtypeStruct(part.shape, BF16) for part in held),
        in_specs=[anywhere] * 3,
        out_specs=[anywhere] * 3,
        scratch_shapes=[dma((len(held),))],
        compiler_params=pltpu.CompilerParams(vmem_limit_bytes=1 << 20),
    )(*held)


def solution(mesh):
    wide = P("section", "ctx", None)
    return jax.shard_map(
        functools.partial(per_device, mesh.shape["section"], mesh.shape["ctx"]),
        mesh=mesh,
        in_specs=(wide, wide, wide, wide, P("section", None), P("section", None, None), P("section", None)),
        out_specs=(wide, wide, wide),
        check_vma=False,
    )
```

profile of v0, /device:TPU:31, one launch (start us, length us, event | category | flops | bytes accessed | tf_op | source)
XLA Modules:
  0.0 40.8 jit_solution(1637668758102264415)
XLA Ops:
  0.6 38.6 %shard_map.94 = (bf16[1,128,8192]{2,1,0:T(8,128)(2,1)S(1)}, bf16[1,128,1024]{2,1,0:T(8,128)(2,1)S(1)}, bf16[1,128,1024]{2,1,0:T(8,128)(2,1)S(1)}) custom-call(bf16[1,128,8192]{2,1,0:T(8,128)(2,1)} %q_hbm.1, bf16[1,128,1024]{2,1,0:T(8,128)(2,1)} %k_hbm.1, bf16[1,128,1024]{2,1,0:T(8,128)(2,1)} %v_hbm.1, bf16[1,128,8192]{2,1,0:T(8,128)(2,1)} %g_hbm.1, ...), custom_call_target="tpu_custom_call" | custom-call | tf_op jit(solution)/shard_map/pallas_call | solution.py:314
  39.3 1.5 %shard_map.95 = (bf16[1,128,8192]{2,1,0:T(8,128)(2,1)}, bf16[1,128,1024]{2,1,0:T(8,128)(2,1)}, bf16[1,128,1024]{2,1,0:T(8,128)(2,1)}) custom-call(bf16[1,128,8192]{2,1,0:T(8,128)(2,1)S(1)} %get-tuple-element.6.held_q, bf16[1,128,1024]{2,1,0:T(8,128)(2,1)S(1)} %get-tuple-element.7.held_k, bf16[1,128,1024]{2,1,0:T(8,128)(2,1)S(1)} %get-tuple-element.8.held_v), custom_call_target="tpu_custom_call" | custom-call | tf_op jit(solution)/shard_map/pallas_call | solution.py:351
where the time goes:
time: 40.9 us; the launch traced here: 40.8 us
  Pallas kernels  40.1 us (98%)
  between operations  0.64 us (2%)
    pallas_call x1, Pallas kernels, per_device(): pl.pallas_call(functools.partial(kernel, section_total, ctx_total), out_s...  38.6 us
    pallas_call x1, Pallas kernels, per_device(): pl.pallas_call(write_out, out_shape=tuple((jax.ShapeDtypeStruct(part.shap...  1.51 us

commit v1 on v0

--- a/solution.py
+++ b/solution.py
@@ -13,7 +13,7 @@
 HEAD_DIM = 128
 BLK = 128
 RATIO = HEADS // KV_HEADS
-PAIR = 2
+PAIR = 4
 WIDTH = RATIO * HEAD_DIM
 
 F32 = jnp.float32
@@ -75,6 +75,8 @@
     after = lax.rem(section + 1, section_total)
 
     def cols(index, width=HEAD_DIM):
+        if isinstance(index, int):
+            return slice(index * width, index * width + width)
         return pl.ds(pl.multiple_of(index * width, width), width)
 
     def block(index):
@@ -212,27 +214,28 @@
                 return jnp.concatenate(parts, axis=0)
 
             def per_pair(pair):
-                here = pl.ds(pl.multiple_of(pair * span, span), span)
-                scores = contract(keys, stacked(q_buf, pair * PAIR, PAIR), 1, 1) * scale
+                here = slice(pair * span, pair * span + span)
+                scores = contract(keys, stacked(q_buf, pair * PAIR, PAIR), 1, 1)
                 masked = bias[0:length, :]
                 scores = scores + jnp.concatenate([masked] * PAIR, axis=1)
-                exponent = jnp.exp(scores - jnp.max(scores, axis=0, keepdims=True))
+                exponent = jnp.exp2((scores - jnp.max(scores, axis=0, keepdims=True)) * (scale * math.log2(math.e)))
                 total = jnp.sum(exponent, axis=0, keepdims=True)
                 attention = exponent * (1.0 / total)
                 at_buf[0:length, here] = attention.astype(BF16)
                 weight_grad = contract(values, stacked(g_buf, pair * PAIR, PAIR), 1, 1)
                 row_delta = jnp.sum(attention * weight_grad, axis=0, keepdims=True)
-                score_grad = (attention * (weight_grad - row_delta) * scale).astype(BF16)
+                score_grad = (attention * (weight_grad - row_delta)).astype(BF16)
                 ds_buf[0:length, here] = score_grad
-                query_grad = contract(score_grad, keys, 0, 0).astype(BF16)
+                query_grad = (contract(score_grad, keys, 0, 0) * scale).astype(BF16)
                 for low in range(PAIR):
                     dq_buf[group, :, cols(pair * PAIR + low)] = query_grad[low * rows : (low + 1) * rows]
-                if late:
-                    pl.when((group == 0) & (pair == 0))(enter)
+                if late and pair == 0:
+                    pl.when(group == 0)(enter)
                 query_copy(group, pair).start()
 
-            pl.loop(0, RATIO // PAIR)(per_pair)
-            key_grad = contract(ds_buf[0:length, :], stacked(q_buf, 0, RATIO), 1, 0)
+            for pair in range(RATIO // PAIR):
+                per_pair(pair)
+            key_grad = contract(ds_buf[0:length, :], stacked(q_buf, 0, RATIO), 1, 0) * scale
             value_grad = contract(at_buf[0:length, :], stacked(g_buf, 0, RATIO), 1, 0)
             first = mine * rows
             if mine > 0:

time: 40.9 us -> 41.6 us (1.017)
  Pallas kernels: 40.1 us -> 40.8 us
    pallas_call x1, Pallas kernels: 38.6 us -> 39.3 us  [per_device(): pl.pallas_call(functools.partial(kernel, section_total, ctx_total), out_s...]
where the time goes in v1:
time: 41.6 us; the launch traced here: 41.4 us
  Pallas kernels  40.8 us (98%)
  between operations  0.64 us (2%)
    pallas_call x1, Pallas kernels, per_device(): pl.pallas_call(functools.partial(kernel, section_total, ctx_total), out_s...  39.3 us
    pallas_call x1, Pallas kernels, per_device(): pl.pallas_call(write_out, out_shape=tuple((jax.ShapeDtypeStruct(part.shap...  1.51 us

profile of v1, /device:TPU:31, one launch (start us, length us, event | category | flops | bytes accessed | tf_op | source)
XLA Modules:
  0.0 41.4 jit_solution(10996638384739640040)
XLA Ops:
  0.6 39.3 %shard_map.94 = (bf16[1,128,8192]{2,1,0:T(8,128)(2,1)S(1)}, bf16[1,128,1024]{2,1,0:T(8,128)(2,1)S(1)}, bf16[1,128,1024]{2,1,0:T(8,128)(2,1)S(1)}) custom-call(bf16[1,128,8192]{2,1,0:T(8,128)(2,1)} %q_hbm.1, bf16[1,128,1024]{2,1,0:T(8,128)(2,1)} %k_hbm.1, bf16[1,128,1024]{2,1,0:T(8,128)(2,1)} %v_hbm.1, bf16[1,128,8192]{2,1,0:T(8,128)(2,1)} %g_hbm.1, ...), custom_call_target="tpu_custom_call" | custom-call | tf_op jit(solution)/shard_map/pallas_call | solution.py:317
  39.9 1.5 %shard_map.95 = (bf16[1,128,8192]{2,1,0:T(8,128)(2,1)}, bf16[1,128,1024]{2,1,0:T(8,128)(2,1)}, bf16[1,128,1024]{2,1,0:T(8,128)(2,1)}) custom-call(bf16[1,128,8192]{2,1,0:T(8,128)(2,1)S(1)} %get-tuple-element.6.held_q, bf16[1,128,1024]{2,1,0:T(8,128)(2,1)S(1)} %get-tuple-element.7.held_k, bf16[1,128,1024]{2,1,0:T(8,128)(2,1)S(1)} %get-tuple-element.8.held_v), custom_call_target="tpu_custom_call" | custom-call | tf_op jit(solution)/shard_map/pallas_call | solution.py:354

commit v2 on v1

--- a/solution.py
+++ b/solution.py
@@ -15,6 +15,8 @@
 RATIO = HEADS // KV_HEADS
 PAIR = 4
 WIDTH = RATIO * HEAD_DIM
+FOLDS = RATIO // 2
+DIAG = 16
 
 F32 = jnp.float32
 BF16 = jnp.bfloat16
@@ -51,6 +53,10 @@
     share,
     shares_in,
     final,
+    fold_out,
+    fold_in,
+    next_keys,
+    relay,
     end_ref,
     list_ref,
     count_ref,
@@ -64,11 +70,17 @@
     share_recv,
     final_send,
     out_recv,
+    fold_send,
+    fold_recv,
+    next_sem,
+    relay_send,
+    relay_recv,
 ):
     rows = q_hbm.shape[1]
     block_total = list_hbm.shape[1]
     blocks_here = rows // BLK
     scale = 1.0 / math.sqrt(HEAD_DIM)
+    last = ctx_total - 1
     section = lax.axis_index("section")
     ctx = lax.axis_index("ctx")
     before = lax.rem(section + section_total - 1, section_total)
@@ -88,6 +100,13 @@
     for step in range(1, ctx_total):
         other = lax.rem(ctx + step, ctx_total)
         pl.semaphore_signal(barrier, 1, device_id={"ctx": other}, device_id_type=MESH)
+    if last > 0:
+
+        @pl.when(ctx == 0)
+        def _():
+            pl.semaphore_signal(
+                barrier, 1, device_id={"section": after, "ctx": last}, device_id_type=MESH
+            )
 
     def load(group):
         for which, source in enumerate((k_hbm, v_hbm)):
@@ -136,6 +155,46 @@
             send_sem=dq_send.at[group],
             recv_sem=out_recv.at[0],
             device_id={"section": before},
+            device_id_type=MESH,
+        )
+
+    def fold_copy(group):
+        return pltpu.make_async_remote_copy(
+            src_ref=fold_out.at[group],
+            dst_ref=fold_in.at[group],
+            send_sem=fold_send.at[group],
+            recv_sem=fold_recv.at[group],
+            device_id={"section": before},
+            device_id_type=MESH,
+        )
+
+    def next_copy():
+        return pltpu.make_async_remote_copy(
+            src_ref=k_hbm.at[0],
+            dst_ref=next_keys,
+            send_sem=next_sem.at[0],
+            recv_sem=next_sem.at[1],
+            device_id={"section": before},
+            device_id_type=MESH,
+        )
+
+    def detour_copy(group, which):
+        return pltpu.make_async_remote_copy(
+            src_ref=final.at[group, which],
+            dst_ref=relay.at[group, which],
+            send_sem=final_send.at[which, group],
+            recv_sem=relay_recv.at[which, group],
+            device_id={"section": before, "ctx": 0},
+            device_id_type=MESH,
+        )
+
+    def relay_copy(group, which):
+        return pltpu.make_async_remote_copy(
+            src_ref=relay.at[group, which],
+            dst_ref=(out_k, out_v)[which].at[0, :, cols(group)],
+            send_sem=relay_send.at[which, group],
+            recv_sem=out_recv.at[1 + which],
+            device_id={"ctx": last},
             device_id_type=MESH,
         )
 
@@ -167,6 +226,42 @@
                     key_block * BLK : (key_block + 1) * BLK, low * BLK : (low + 1) * BLK
                 ] = jnp.where(allowed, 0.0, -jnp.inf).astype(F32).T
 
+    def corner():
+        down = lax.broadcasted_iota(jnp.int32, (rows, rows), 0)
+        across = lax.broadcasted_iota(jnp.int32, (rows, rows), 1)
+        return down, across
+
+    def fold(group, score_float):
+        down, across = corner()
+        place = lax.broadcasted_iota(jnp.int32, (DIAG, rows), 0)
+        diagonals = jnp.zeros((DIAG, rows), F32)
+        for pair in range(FOLDS):
+            upper = score_float[:, 2 * pair * rows : (2 * pair + 1) * rows]
+            other = score_float[:, (2 * pair + 1) * rows : (2 * pair + 2) * rows]
+            square = jnp.where(down <= across, upper, other.T)
+            fold_out[group, pair * rows : (pair + 1) * rows, :] = square.astype(BF16)
+            diagonal = jnp.sum(jnp.where(down == across, other, 0.0), axis=0, keepdims=True)
+            diagonals = jnp.where(place == pair, diagonal, diagonals)
+        fold_out[group, FOLDS * rows :, :] = diagonals.astype(BF16)
+
+    def unfold(group):
+        down, across = corner()
+        keys = next_keys[:, cols(group)]
+        diagonals = fold_in[group, FOLDS * rows :, :].astype(F32)
+        uppers, lowers = [], []
+        for pair in range(FOLDS):
+            square = fold_in[group, pair * rows : (pair + 1) * rows, :].astype(F32)
+            diagonal = diagonals[pair : pair + 1, :]
+            uppers.append(jnp.where(down <= across, square, 0.0).astype(BF16))
+            rest = jnp.where(down == across, diagonal, 0.0)
+            lowers.append(jnp.where(down > across, square, rest).astype(BF16))
+        even = contract(jnp.concatenate(uppers, axis=1), keys, 0, 0).astype(BF16)
+        odd = contract(jnp.concatenate(lowers, axis=0), keys, 1, 0).astype(BF16)
+        for pair in range(FOLDS):
+            here = slice(pair * rows, (pair + 1) * rows)
+            out_q[0, :, cols(group * RATIO + 2 * pair)] = even[here]
+            out_q[0, :, cols(group * RATIO + 2 * pair + 1)] = odd[here]
+
     def run(mine):
         length = (mine + 1) * rows
         for table in tables:
@@ -180,14 +275,17 @@
                     kv_copy(group, which, mine, peer).start()
 
         def enter():
-            pl.semaphore_wait(barrier, 1 + ctx_total)
-            if mine < ctx_total - 1:
+            pl.semaphore_wait(barrier, 1 + ctx_total + (1 if 0 < mine == last else 0))
+            if mine < last:
                 pl.when(section % 2 == 0)(lambda: send_keys(0))
-
-        late = mine == ctx_total - 1
+            if mine == 0:
+                next_copy().start()
+
+        late = 0 < mine == last
         if not late:
             enter()
-        span = PAIR * rows
+        heads = RATIO if mine == 0 else PAIR
+        span = heads * rows
 
         def per_group(group, carry):
             if mine < ctx_total - 1:
@@ -215,27 +313,33 @@
 
             def per_pair(pair):
                 here = slice(pair * span, pair * span + span)
-                scores = contract(keys, stacked(q_buf, pair * PAIR, PAIR), 1, 1)
+                scores = contract(keys, stacked(q_buf, pair * heads, heads), 1, 1)
                 masked = bias[0:length, :]
-                scores = scores + jnp.concatenate([masked] * PAIR, axis=1)
-                exponent = jnp.exp2((scores - jnp.max(scores, axis=0, keepdims=True)) * (scale * math.log2(math.e)))
+                scores = scores + jnp.concatenate([masked] * heads, axis=1)
+                shifted = scores - jnp.max(scores, axis=0, keepdims=True)
+                exponent = jnp.exp2(shifted * (scale * math.log2(math.e)))
                 total = jnp.sum(exponent, axis=0, keepdims=True)
                 attention = exponent * (1.0 / total)
                 at_buf[0:length, here] = attention.astype(BF16)
-                weight_grad = contract(values, stacked(g_buf, pair * PAIR, PAIR), 1, 1)
+                weight_grad = contract(values, stacked(g_buf, pair * heads, heads), 1, 1)
                 row_delta = jnp.sum(attention * weight_grad, axis=0, keepdims=True)
-                score_grad = (attention * (weight_grad - row_delta)).astype(BF16)
+                score_float = attention * (weight_grad - row_delta) * scale
+                score_grad = score_float.astype(BF16)
                 ds_buf[0:length, here] = score_grad
-                query_grad = (contract(score_grad, keys, 0, 0) * scale).astype(BF16)
-                for low in range(PAIR):
-                    dq_buf[group, :, cols(pair * PAIR + low)] = query_grad[low * rows : (low + 1) * rows]
+                if mine == 0:
+                    fold(group, score_float)
+                    fold_copy(group).start()
+                    return
+                query_grad = contract(score_grad, keys, 0, 0).astype(BF16)
+                for low in range(heads):
+                    dq_buf[group, :, cols(pair * heads + low)] = query_grad[low * rows : (low + 1) * rows]
                 if late and pair == 0:
                     pl.when(group == 0)(enter)
                 query_copy(group, pair).start()
 
-            for pair in range(RATIO // PAIR):
+            for pair in range(RATIO // heads):
                 per_pair(pair)
-            key_grad = contract(ds_buf[0:length, :], stacked(q_buf, 0, RATIO), 1, 0) * scale
+            key_grad = contract(ds_buf[0:length, :], stacked(q_buf, 0, RATIO), 1, 0)
             value_grad = contract(at_buf[0:length, :], stacked(g_buf, 0, RATIO), 1, 0)
             first = mine * rows
             if mine > 0:
@@ -247,7 +351,11 @@
                 final[group, 0] = key_grad[first:].astype(BF16)
                 final[group, 1] = value_grad[first:].astype(BF16)
                 for which in range(2):
-                    final_copy(group, which).start()
+                    if mine > 0:
+                        pl.when(section % 2 == 0)(detour_copy(group, which).start)
+                        pl.when(section % 2 == 1)(final_copy(group, which).start)
+                    else:
+                        final_copy(group, which).start()
             else:
                 own[group, 0] = key_grad[first:]
                 own[group, 1] = value_grad[first:]
@@ -255,10 +363,14 @@
 
         lax.fori_loop(0, KV_HEADS, per_group, 0)
 
-        if mine < ctx_total - 1:
-
-            @pl.loop(0, KV_HEADS)
-            def _(group):
+        if mine == 0:
+            next_copy().wait_recv()
+
+        def finish(group):
+            if mine == 0:
+                fold_copy(group).wait_recv()
+                unfold(group)
+            if mine < last:
                 total = own[group]
                 for source in range(mine + 1, ctx_total):
                     share_copy(group, source, mine).wait_recv()
@@ -266,6 +378,16 @@
                 final[group] = total.astype(BF16)
                 for which in range(2):
                     final_copy(group, which).start()
+            if mine == 0 and last > 0:
+
+                @pl.when(after % 2 == 0)
+                def _():
+                    for which in range(2):
+                        detour_copy(group, which).wait_recv()
+                        relay_copy(group, which).start()
+
+        if mine < last or mine == 0:
+            pl.loop(0, KV_HEADS)(finish)
 
         @pl.loop(0, KV_HEADS)
         def _(group):
@@ -274,17 +396,28 @@
                     kv_copy(group, which, mine, peer).wait_send()
             for peer in range(mine):
                 share_copy(group, mine, peer).wait_send()
+            for which in range(2):
+                final_copy(group, which).wait_send()
+            if mine > 0:
+                pltpu.make_async_copy(dq_buf.at[group], dq_buf.at[group], dq_send.at[group]).wait()
+            else:
+                fold_copy(group).wait_send()
+            if mine == 0 and last > 0:
+
+                @pl.when(after % 2 == 0)
+                def _():
+                    for which in range(2):
+                        relay_copy(group, which).wait_send()
+
+        if mine == 0:
+            next_copy().wait_send()
+        else:
+            pltpu.make_async_copy(out_q, out_q, out_recv.at[0]).wait()
 
     for mine in range(ctx_total):
         pl.when(ctx == mine)(functools.partial(run, mine))
 
-    @pl.loop(0, KV_HEADS)
-    def _(group):
-        pltpu.make_async_copy(dq_buf.at[group], dq_buf.at[group], dq_send.at[group]).wait()
-        for which in range(2):
-            final_copy(group, which).wait_send()
-
-    for slot, out in enumerate((out_q, out_k, out_v)):
+    for slot, out in ((1, out_k), (2, out_v)):
         pltpu.make_async_copy(out, out, out_recv.at[slot]).wait()
 
 
@@ -335,6 +468,10 @@
             pltpu.VMEM((KV_HEADS, 2, length, HEAD_DIM), BF16),
             pltpu.VMEM((KV_HEADS, ctx_total, 2, rows, HEAD_DIM), BF16),
             pltpu.VMEM((KV_HEADS, 2, rows, HEAD_DIM), BF16),
+            pltpu.VMEM((KV_HEADS, FOLDS * rows + DIAG, rows), BF16),
+            pltpu.VMEM((KV_HEADS, FOLDS * rows + DIAG, rows), BF16),
+            pltpu.VMEM((rows, KV_HEADS * HEAD_DIM), BF16),
+            pltpu.VMEM((KV_HEADS, 2, rows, HEAD_DIM), BF16),
             pltpu.VMEM(node_end.shape, jnp.int32),
             pltpu.SMEM(block_list.shape, jnp.int32),
             pltpu.SMEM(block_count.shape, jnp.int32),
@@ -348,6 +485,11 @@
             dma((ctx_total, KV_HEADS)),
             dma((2, KV_HEADS)),
             dma((3,)),
+            dma((KV_HEADS,)),
+            dma((KV_HEADS,)),
+            dma((2,)),
+            dma((2, KV_HEADS)),
+            dma((2, KV_HEADS)),
         ],
         compiler_params=pltpu.CompilerParams(collective_id=0, has_side_effects=True),
     )(queries, key_states, value_states, out_grad, node_end, block_list, block_count)

time: 41.6 us -> 44.7 us (1.075)
  Pallas kernels: 40.8 us -> 43.9 us
    pallas_call x1, Pallas kernels: 39.3 us -> 42.4 us  [per_device(): pl.pallas_call(functools.partial(kernel, section_total, ctx_total), out_s...]
where the time goes in v2:
time: 44.7 us; the launch traced here: 44.6 us
  Pallas kernels  43.9 us (98%)
  between operations  0.64 us (1%)
    pallas_call x1, Pallas kernels, per_device(): pl.pallas_call(functools.partial(kernel, section_total, ctx_total), out_s...  42.4 us
    pallas_call x1, Pallas kernels, per_device(): pl.pallas_call(write_out, out_shape=tuple((jax.ShapeDtypeStruct(part.shap...  1.51 us

profile of v2, /device:TPU:31, one launch (start us, length us, event | category | flops | bytes accessed | tf_op | source)
XLA Modules:
  0.0 44.6 jit_solution(3689360026191384604)
XLA Ops:
  0.6 42.4 %shard_map.94 = (bf16[1,128,8192]{2,1,0:T(8,128)(2,1)S(1)}, bf16[1,128,1024]{2,1,0:T(8,128)(2,1)S(1)}, bf16[1,128,1024]{2,1,0:T(8,128)(2,1)S(1)}) custom-call(bf16[1,128,8192]{2,1,0:T(8,128)(2,1)} %q_hbm.1, bf16[1,128,1024]{2,1,0:T(8,128)(2,1)} %k_hbm.1, bf16[1,128,1024]{2,1,0:T(8,128)(2,1)} %v_hbm.1, bf16[1,128,8192]{2,1,0:T(8,128)(2,1)} %g_hbm.1, ...), custom_call_target="tpu_custom_call" | custom-call | tf_op jit(solution)/shard_map/pallas_call | solution.py:450
  43.1 1.5 %shard_map.95 = (bf16[1,128,8192]{2,1,0:T(8,128)(2,1)}, bf16[1,128,1024]{2,1,0:T(8,128)(2,1)}, bf16[1,128,1024]{2,1,0:T(8,128)(2,1)}) custom-call(bf16[1,128,8192]{2,1,0:T(8,128)(2,1)S(1)} %get-tuple-element.6.held_q, bf16[1,128,1024]{2,1,0:T(8,128)(2,1)S(1)} %get-tuple-element.7.held_k, bf16[1,128,1024]{2,1,0:T(8,128)(2,1)S(1)} %get-tuple-element.8.held_v), custom_call_target="tpu_custom_call" | custom-call | tf_op jit(solution)/shard_map/pallas_call | solution.py:496

commit v3 on v2

--- a/solution.py
+++ b/solution.py
@@ -56,6 +56,7 @@
     fold_out,
     fold_in,
     next_keys,
+    aside,
     relay,
     end_ref,
     list_ref,
@@ -73,6 +74,8 @@
     fold_send,
     fold_recv,
     next_sem,
+    aside_send,
+    aside_recv,
     relay_send,
     relay_recv,
 ):
@@ -100,14 +103,6 @@
     for step in range(1, ctx_total):
         other = lax.rem(ctx + step, ctx_total)
         pl.semaphore_signal(barrier, 1, device_id={"ctx": other}, device_id_type=MESH)
-    if last > 0:
-
-        @pl.when(ctx == 0)
-        def _():
-            pl.semaphore_signal(
-                barrier, 1, device_id={"section": after, "ctx": last}, device_id_type=MESH
-            )
-
     def load(group):
         for which, source in enumerate((k_hbm, v_hbm)):
             pltpu.make_async_copy(
@@ -178,13 +173,23 @@
             device_id_type=MESH,
         )
 
+    def aside_copy(group, which):
+        return pltpu.make_async_remote_copy(
+            src_ref=final.at[group, which],
+            dst_ref=aside.at[group, which],
+            send_sem=final_send.at[which, group],
+            recv_sem=aside_recv.at[which, group],
+            device_id={"ctx": 0},
+            device_id_type=MESH,
+        )
+
     def detour_copy(group, which):
         return pltpu.make_async_remote_copy(
-            src_ref=final.at[group, which],
+            src_ref=aside.at[group, which],
             dst_ref=relay.at[group, which],
-            send_sem=final_send.at[which, group],
+            send_sem=aside_send.at[which, group],
             recv_sem=relay_recv.at[which, group],
-            device_id={"section": before, "ctx": 0},
+            device_id={"section": before},
             device_id_type=MESH,
         )
 
@@ -275,7 +280,7 @@
                     kv_copy(group, which, mine, peer).start()
 
         def enter():
-            pl.semaphore_wait(barrier, 1 + ctx_total + (1 if 0 < mine == last else 0))
+            pl.semaphore_wait(barrier, 1 + ctx_total)
             if mine < last:
                 pl.when(section % 2 == 0)(lambda: send_keys(0))
             if mine == 0:
@@ -352,7 +357,7 @@
                 final[group, 1] = value_grad[first:].astype(BF16)
                 for which in range(2):
                     if mine > 0:
-                        pl.when(section % 2 == 0)(detour_copy(group, which).start)
+                        pl.when(section % 2 == 0)(aside_copy(group, which).start)
                         pl.when(section % 2 == 1)(final_copy(group, which).start)
                     else:
                         final_copy(group, which).start()
@@ -365,6 +370,16 @@
 
         if mine == 0:
             next_copy().wait_recv()
+
+        def forward(group):
+            for which in range(2):
+                aside_copy(group, which).wait_recv()
+                detour_copy(group, which).start()
+
+        def hand_over(group):
+            for which in range(2):
+                detour_copy(group, which).wait_recv()
+                relay_copy(group, which).start()
 
         def finish(group):
             if mine == 0:
@@ -379,15 +394,13 @@
                 for which in range(2):
                     final_copy(group, which).start()
             if mine == 0 and last > 0:
-
-                @pl.when(after % 2 == 0)
-                def _():
-                    for which in range(2):
-                        detour_copy(group, which).wait_recv()
-                        relay_copy(group, which).start()
+                pl.when(section % 2 == 0)(lambda: forward(group))
+                pl.when((after % 2 == 0) & (group > 0))(lambda: hand_over(group - 1))
 
         if mine < last or mine == 0:
             pl.loop(0, KV_HEADS)(finish)
+        if mine == 0 and last > 0:
+            pl.when(after % 2 == 0)(lambda: hand_over(KV_HEADS - 1))
 
         @pl.loop(0, KV_HEADS)
         def _(group):
@@ -408,6 +421,11 @@
                 def _():
                     for which in range(2):
                         relay_copy(group, which).wait_send()
+
+                @pl.when(section % 2 == 0)
+                def _():
+                    for which in range(2):
+                        detour_copy(group, which).wait_send()
 
         if mine == 0:
             next_copy().wait_send()
@@ -472,6 +490,7 @@
             pltpu.VMEM((KV_HEADS, FOLDS * rows + DIAG, rows), BF16),
             pltpu.VMEM((rows, KV_HEADS * HEAD_DIM), BF16),
             pltpu.VMEM((KV_HEADS, 2, rows, HEAD_DIM), BF16),
+            pltpu.VMEM((KV_HEADS, 2, rows, HEAD_DIM), BF16),
             pltpu.VMEM(node_end.shape, jnp.int32),
             pltpu.SMEM(block_list.shape, jnp.int32),
             pltpu.SMEM(block_count.shape, jnp.int32),
@@ -490,6 +509,8 @@
             dma((2,)),
             dma((2, KV_HEADS)),
             dma((2, KV_HEADS)),
+            dma((2, KV_HEADS)),
+            dma((2, KV_HEADS)),
         ],
         compiler_params=pltpu.CompilerParams(collective_id=0, has_side_effects=True),
     )(queries, key_states, value_states, out_grad, node_end, block_list, block_count)

time: 44.7 us -> 37.4 us (0.84)
  Pallas kernels: 43.9 us -> 36.6 us
    pallas_call x1, Pallas kernels: 42.4 us -> 35.1 us  [per_device(): pl.pallas_call(functools.partial(kernel, section_total, ctx_total), out_s...]
where the time goes in v3:
time: 37.4 us; the launch traced here: 37.2 us
  Pallas kernels  36.6 us (98%)
  between operations  0.64 us (2%)
    pallas_call x1, Pallas kernels, per_device(): pl.pallas_call(functools.partial(kernel, section_total, ctx_total), out_s...  35.1 us
    pallas_call x1, Pallas kernels, per_device(): pl.pallas_call(write_out, out_shape=tuple((jax.ShapeDtypeStruct(part.shap...  1.51 us

profile of v3, /device:TPU:31, one launch (start us, length us, event | category | flops | bytes accessed | tf_op | source)
XLA Modules:
  0.0 37.2 jit_solution(12837982970743202123)
XLA Ops:
  0.6 35.1 %shard_map.94 = (bf16[1,128,8192]{2,1,0:T(8,128)(2,1)S(1)}, bf16[1,128,1024]{2,1,0:T(8,128)(2,1)S(1)}, bf16[1,128,1024]{2,1,0:T(8,128)(2,1)S(1)}) custom-call(bf16[1,128,8192]{2,1,0:T(8,128)(2,1)} %q_hbm.1, bf16[1,128,1024]{2,1,0:T(8,128)(2,1)} %k_hbm.1, bf16[1,128,1024]{2,1,0:T(8,128)(2,1)} %v_hbm.1, bf16[1,128,8192]{2,1,0:T(8,128)(2,1)} %g_hbm.1, ...), custom_call_target="tpu_custom_call" | custom-call | tf_op jit(solution)/shard_map/pallas_call | solution.py:468
  35.7 1.5 %shard_map.95 = (bf16[1,128,8192]{2,1,0:T(8,128)(2,1)}, bf16[1,128,1024]{2,1,0:T(8,128)(2,1)}, bf16[1,128,1024]{2,1,0:T(8,128)(2,1)}) custom-call(bf16[1,128,8192]{2,1,0:T(8,128)(2,1)S(1)} %get-tuple-element.6.held_q, bf16[1,128,1024]{2,1,0:T(8,128)(2,1)S(1)} %get-tuple-element.7.held_k, bf16[1,128,1024]{2,1,0:T(8,128)(2,1)S(1)} %get-tuple-element.8.held_v), custom_call_target="tpu_custom_call" | custom-call | tf_op jit(solution)/shard_map/pallas_call | solution.py:517

commit v4 on v3

--- a/solution.py
+++ b/solution.py
@@ -17,6 +17,8 @@
 WIDTH = RATIO * HEAD_DIM
 FOLDS = RATIO // 2
 DIAG = 16
+DIRECT = 1
+DIRECT_WRAP = 2
 
 F32 = jnp.float32
 BF16 = jnp.bfloat16
@@ -78,6 +80,7 @@
     aside_recv,
     relay_send,
     relay_recv,
+    ready,
 ):
     rows = q_hbm.shape[1]
     block_total = list_hbm.shape[1]
@@ -89,6 +92,10 @@
     before = lax.rem(section + section_total - 1, section_total)
     after = lax.rem(section + 1, section_total)
 
+    def detoured(source, group):
+        direct = jnp.where(source == 0, DIRECT_WRAP, DIRECT)
+        return (source % 2 == 0) & (group < KV_HEADS - direct)
+
     def cols(index, width=HEAD_DIM):
         if isinstance(index, int):
             return slice(index * width, index * width + width)
@@ -98,8 +105,12 @@
         return pl.ds(pl.multiple_of(index * rows, rows), rows)
 
     barrier = pltpu.get_barrier_semaphore()
-    for target in (before, after):
-        pl.semaphore_signal(barrier, 1, device_id={"section": target}, device_id_type=MESH)
+
+    @pl.when(section % 2 == 0)
+    def _():
+        for target in (before, after):
+            pl.semaphore_signal(barrier, 1, device_id={"section": target}, device_id_type=MESH)
+
     for step in range(1, ctx_total):
         other = lax.rem(ctx + step, ctx_total)
         pl.semaphore_signal(barrier, 1, device_id={"ctx": other}, device_id_type=MESH)
@@ -269,44 +280,63 @@
 
     def run(mine):
         length = (mine + 1) * rows
+        def send_keys(group):
+            for peer in range(mine + 1, ctx_total):
+                for which in range(2):
+                    kv_copy(group, which, mine, peer).start()
+
+        def enter():
+            @pl.when(section % 2 == 0)
+            def _():
+                if ctx_total > 1:
+                    pl.semaphore_wait(barrier, ctx_total - 1)
+
+            @pl.when(section % 2 == 1)
+            def _():
+                pl.semaphore_wait(barrier, ctx_total + 1)
+                pl.semaphore_signal(ready, 1, device_id={"section": after}, device_id_type=MESH)
+
+        def reach():
+            pl.when(section % 2 == 0)(lambda: pl.semaphore_wait(ready, 1))
+            if mine == 0:
+                next_copy().start()
+
+        def wait_own(group):
+            pltpu.make_async_copy(
+                kv_buf.at[group, :, pl.ds(mine * rows, rows)],
+                kv_buf.at[group, :, pl.ds(mine * rows, rows)],
+                kv_sem.at[group],
+            ).wait()
+
+        def lead(group):
+            if mine < last:
+                pl.when(section % 2 == 0)(lambda: send_keys(group))
+
+        late = 0 < mine == last
+        enter()
+        if not late:
+            lead(0)
         for table in tables:
             table.wait()
         fill_bias((mine + 1) * blocks_here)
         pl.loop(1, KV_HEADS)(load)
-
-        def send_keys(group):
-            for peer in range(mine + 1, ctx_total):
-                for which in range(2):
-                    kv_copy(group, which, mine, peer).start()
-
-        def enter():
-            pl.semaphore_wait(barrier, 1 + ctx_total)
-            if mine < last:
-                pl.when(section % 2 == 0)(lambda: send_keys(0))
-            if mine == 0:
-                next_copy().start()
-
-        late = 0 < mine == last
-        if not late:
-            enter()
+        if mine == 0:
+            pl.when(section > 0)(reach)
         heads = RATIO if mine == 0 else PAIR
         span = heads * rows
 
         def per_group(group, carry):
-            if mine < ctx_total - 1:
-                pl.when((section % 2 == 0) & (group + 1 < KV_HEADS))(lambda: send_keys(group + 1))
-                pl.when(section % 2 == 1)(lambda: send_keys(group))
+            wait_own(group)
+            if not late:
+                pl.when(group > 0)(lambda: lead(group))
+            if mine < last:
+                pl.when((section % 2 == 1) & (group > 0))(lambda: send_keys(group - 1))
             for source in range(mine):
                 pltpu.make_async_copy(
                     kv_buf.at[group, :, pl.ds(source * rows, rows)],
                     kv_buf.at[group, :, pl.ds(source * rows, rows)],
                     kv_recv.at[source, group],
                 ).wait()
-            pltpu.make_async_copy(
-                kv_buf.at[group, :, pl.ds(mine * rows, rows)],
-                kv_buf.at[group, :, pl.ds(mine * rows, rows)],
-                kv_sem.at[group],
-            ).wait()
             pltpu.make_async_copy(q_buf.at[group], q_buf.at[group], load_sem.at[0, group]).wait()
             pltpu.make_async_copy(g_buf.at[group], g_buf.at[group], load_sem.at[1, group]).wait()
             keys = kv_buf[group, 0, 0:length, :]
@@ -333,13 +363,14 @@
                 ds_buf[0:length, here] = score_grad
                 if mine == 0:
                     fold(group, score_float)
+                    pl.when((group == 0) & (section == 0))(reach)
                     fold_copy(group).start()
                     return
                 query_grad = contract(score_grad, keys, 0, 0).astype(BF16)
                 for low in range(heads):
                     dq_buf[group, :, cols(pair * heads + low)] = query_grad[low * rows : (low + 1) * rows]
-                if late and pair == 0:
-                    pl.when(group == 0)(enter)
+                if mine > 0 and pair == 0:
+                    pl.when(group == 0)(reach)
                 query_copy(group, pair).start()
 
             for pair in range(RATIO // heads):
@@ -347,26 +378,29 @@
             key_grad = contract(ds_buf[0:length, :], stacked(q_buf, 0, RATIO), 1, 0)
             value_grad = contract(at_buf[0:length, :], stacked(g_buf, 0, RATIO), 1, 0)
             first = mine * rows
+            if mine == last:
+                final[group, 0] = key_grad[first:].astype(BF16)
+                final[group, 1] = value_grad[first:].astype(BF16)
+                for which in range(2):
+                    if mine > 0:
+                        by_side = detoured(section, group)
+                        pl.when(by_side)(aside_copy(group, which).start)
+                        pl.when(jnp.logical_not(by_side))(final_copy(group, which).start)
+                    else:
+                        final_copy(group, which).start()
+            else:
+                own[group, 0] = key_grad[first:]
+                own[group, 1] = value_grad[first:]
             if mine > 0:
                 share[group, 0, 0:first, :] = key_grad[0:first].astype(BF16)
                 share[group, 1, 0:first, :] = value_grad[0:first].astype(BF16)
                 for peer in range(mine):
                     share_copy(group, mine, peer).start()
-            if mine == ctx_total - 1:
-                final[group, 0] = key_grad[first:].astype(BF16)
-                final[group, 1] = value_grad[first:].astype(BF16)
-                for which in range(2):
-                    if mine > 0:
-                        pl.when(section % 2 == 0)(aside_copy(group, which).start)
-                        pl.when(section % 2 == 1)(final_copy(group, which).start)
-                    else:
-                        final_copy(group, which).start()
-            else:
-                own[group, 0] = key_grad[first:]
-                own[group, 1] = value_grad[first:]
             return carry
 
         lax.fori_loop(0, KV_HEADS, per_group, 0)
+        if mine < last:
+            pl.when(section % 2 == 1)(lambda: send_keys(KV_HEADS - 1))
 
         if mine == 0:
             next_copy().wait_recv()
@@ -394,13 +428,12 @@
                 for which in range(2):
                     final_copy(group, which).start()
             if mine == 0 and last > 0:
-                pl.when(section % 2 == 0)(lambda: forward(group))
-                pl.when((after % 2 == 0) & (group > 0))(lambda: hand_over(group - 1))
+                pl.when(detoured(section, group))(lambda: forward(group))
+                handed = (group > 0) & detoured(after, group - 1)
+                pl.when(handed)(lambda: hand_over(group - 1))
 
         if mine < last or mine == 0:
             pl.loop(0, KV_HEADS)(finish)
-        if mine == 0 and last > 0:
-            pl.when(after % 2 == 0)(lambda: hand_over(KV_HEADS - 1))
 
         @pl.loop(0, KV_HEADS)
         def _(group):
@@ -417,12 +450,12 @@
                 fold_copy(group).wait_send()
             if mine == 0 and last > 0:
 
-                @pl.when(after % 2 == 0)
+                @pl.when(detoured(after, group))
                 def _():
                     for which in range(2):
                         relay_copy(group, which).wait_send()
 
-                @pl.when(section % 2 == 0)
+                @pl.when(detoured(section, group))
                 def _():
                     for which in range(2):
                         detour_copy(group, which).wait_send()
@@ -511,6 +544,7 @@
             dma((2, KV_HEADS)),
             dma((2, KV_HEADS)),
             dma((2, KV_HEADS)),
+            pltpu.SemaphoreType.REGULAR,
         ],
         compiler_params=pltpu.CompilerParams(collective_id=0, has_side_effects=True),
     )(queries, key_states, value_states, out_grad, node_end, block_list, block_count)

time: 37.4 us -> 36.9 us (0.987)
  Pallas kernels: 36.6 us -> 36.1 us
    pallas_call x1, Pallas kernels: 35.1 us -> 34.6 us  [per_device(): pl.pallas_call(functools.partial(kernel, section_total, ctx_total), out_s...]
where the time goes in v4:
time: 36.9 us; the launch traced here: 36.7 us
  Pallas kernels  36.1 us (98%)
  between operations  0.64 us (2%)
    pallas_call x1, Pallas kernels, per_device(): pl.pallas_call(functools.partial(kernel, section_total, ctx_total), out_s...  34.6 us
    pallas_call x1, Pallas kernels, per_device(): pl.pallas_call(write_out, out_shape=tuple((jax.ShapeDtypeStruct(part.shap...  1.51 us

profile of v4, /device:TPU:31, one launch (start us, length us, event | category | flops | bytes accessed | tf_op | source)
XLA Modules:
  0.0 36.7 jit_solution(2453815089580590813)
XLA Ops:
  0.6 34.6 %shard_map.94 = (bf16[1,128,8192]{2,1,0:T(8,128)(2,1)S(1)}, bf16[1,128,1024]{2,1,0:T(8,128)(2,1)S(1)}, bf16[1,128,1024]{2,1,0:T(8,128)(2,1)S(1)}) custom-call(bf16[1,128,8192]{2,1,0:T(8,128)(2,1)} %q_hbm.1, bf16[1,128,1024]{2,1,0:T(8,128)(2,1)} %k_hbm.1, bf16[1,128,1024]{2,1,0:T(8,128)(2,1)} %v_hbm.1, bf16[1,128,8192]{2,1,0:T(8,128)(2,1)} %g_hbm.1, ...), custom_call_target="tpu_custom_call" | custom-call | tf_op jit(solution)/shard_map/pallas_call | solution.py:501
  35.2 1.5 %shard_map.95 = (bf16[1,128,8192]{2,1,0:T(8,128)(2,1)}, bf16[1,128,1024]{2,1,0:T(8,128)(2,1)}, bf16[1,128,1024]{2,1,0:T(8,128)(2,1)}) custom-call(bf16[1,128,8192]{2,1,0:T(8,128)(2,1)S(1)} %get-tuple-element.6.held_q, bf16[1,128,1024]{2,1,0:T(8,128)(2,1)S(1)} %get-tuple-element.7.held_k, bf16[1,128,1024]{2,1,0:T(8,128)(2,1)S(1)} %get-tuple-element.8.held_v), custom_call_target="tpu_custom_call" | custom-call | tf_op jit(solution)/shard_map/pallas_call | solution.py:551

commit v5 on v4

--- a/solution.py
+++ b/solution.py
@@ -13,7 +13,8 @@
 HEAD_DIM = 128
 BLK = 128
 RATIO = HEADS // KV_HEADS
-PAIR = 4
+STEPS = (4, 4)
+FIRST_STEPS = (2, 2, 4)
 WIDTH = RATIO * HEAD_DIM
 FOLDS = RATIO // 2
 DIAG = 16
@@ -154,10 +155,13 @@
             device_id_type=MESH,
         )
 
-    def query_copy(group, pair):
-        return pltpu.make_async_remote_copy(
-            src_ref=dq_buf.at[group, :, cols(pair, PAIR * HEAD_DIM)],
-            dst_ref=out_q.at[0, :, cols(group * (RATIO // PAIR) + pair, PAIR * HEAD_DIM)],
+    def query_copy(group, first, count):
+        start = group * WIDTH + first * HEAD_DIM
+        if not isinstance(group, int):
+            start = pl.multiple_of(start, HEAD_DIM)
+        return pltpu.make_async_remote_copy(
+            src_ref=dq_buf.at[group, :, first * HEAD_DIM : (first + count) * HEAD_DIM],
+            dst_ref=out_q.at[0, :, pl.ds(start, count * HEAD_DIM)],
             send_sem=dq_send.at[group],
             recv_sem=out_recv.at[0],
             device_id={"section": before},
@@ -296,6 +300,12 @@
                 pl.semaphore_wait(barrier, ctx_total + 1)
                 pl.semaphore_signal(ready, 1, device_id={"section": after}, device_id_type=MESH)
 
+        def when_first(group, action):
+            if not isinstance(group, int):
+                pl.when(group == 0)(action)
+            elif group == 0:
+                action()
+
         def reach():
             pl.when(section % 2 == 0)(lambda: pl.semaphore_wait(ready, 1))
             if mine == 0:
@@ -322,10 +332,9 @@
         pl.loop(1, KV_HEADS)(load)
         if mine == 0:
             pl.when(section > 0)(reach)
-        heads = RATIO if mine == 0 else PAIR
-        span = heads * rows
-
-        def per_group(group, carry):
+        usual = (RATIO,) if mine == 0 else STEPS
+
+        def per_group(group, carry, steps=usual):
             wait_own(group)
             if not late:
                 pl.when(group > 0)(lambda: lead(group))
@@ -346,9 +355,9 @@
                 parts = [ref[group, :, cols(first + low)] for low in range(count)]
                 return jnp.concatenate(parts, axis=0)
 
-            def per_pair(pair):
-                here = slice(pair * span, pair * span + span)
-                scores = contract(keys, stacked(q_buf, pair * heads, heads), 1, 1)
+            def per_step(start, heads):
+                here = slice(start * rows, (start + heads) * rows)
+                scores = contract(keys, stacked(q_buf, start, heads), 1, 1)
                 masked = bias[0:length, :]
                 scores = scores + jnp.concatenate([masked] * heads, axis=1)
                 shifted = scores - jnp.max(scores, axis=0, keepdims=True)
@@ -356,7 +365,7 @@
                 total = jnp.sum(exponent, axis=0, keepdims=True)
                 attention = exponent * (1.0 / total)
                 at_buf[0:length, here] = attention.astype(BF16)
-                weight_grad = contract(values, stacked(g_buf, pair * heads, heads), 1, 1)
+                weight_grad = contract(values, stacked(g_buf, start, heads), 1, 1)
                 row_delta = jnp.sum(attention * weight_grad, axis=0, keepdims=True)
                 score_float = attention * (weight_grad - row_delta) * scale
                 score_grad = score_float.astype(BF16)
@@ -368,13 +377,13 @@
                     return
                 query_grad = contract(score_grad, keys, 0, 0).astype(BF16)
                 for low in range(heads):
-                    dq_buf[group, :, cols(pair * heads + low)] = query_grad[low * rows : (low + 1) * rows]
-                if mine > 0 and pair == 0:
-                    pl.when(group == 0)(reach)
-                query_copy(group, pair).start()
-
-            for pair in range(RATIO // heads):
-                per_pair(pair)
+                    dq_buf[group, :, cols(start + low)] = query_grad[low * rows : (low + 1) * rows]
+                if mine > 0 and start == 0:
+                    when_first(group, reach)
+                query_copy(group, start, heads).start()
+
+            for step, heads in enumerate(steps):
+                per_step(sum(steps[:step]), heads)
             key_grad = contract(ds_buf[0:length, :], stacked(q_buf, 0, RATIO), 1, 0)
             value_grad = contract(at_buf[0:length, :], stacked(g_buf, 0, RATIO), 1, 0)
             first = mine * rows
@@ -398,7 +407,9 @@
                     share_copy(group, mine, peer).start()
             return carry
 
-        lax.fori_loop(0, KV_HEADS, per_group, 0)
+        if late:
+            per_group(0, 0, FIRST_STEPS)
+        lax.fori_loop(int(late), KV_HEADS, per_group, 0)
         if mine < last:
             pl.when(section % 2 == 1)(lambda: send_keys(KV_HEADS - 1))
 

time: 36.9 us -> 36.9 us (level)
  no operation moved by 1% of the time
where the time goes in v5:
time: 36.9 us; the launch traced here: 36.7 us
  Pallas kernels  36.1 us (98%)
  between operations  0.64 us (2%)
    pallas_call x1, Pallas kernels, per_device(): pl.pallas_call(functools.partial(kernel, section_total, ctx_total), out_s...  34.6 us
    pallas_call x1, Pallas kernels, per_device(): pl.pallas_call(write_out, out_shape=tuple((jax.ShapeDtypeStruct(part.shap...  1.51 us

profile of v5, /device:TPU:31, one launch (start us, length us, event | category | flops | bytes accessed | tf_op | source)
XLA Modules:
  0.0 36.7 jit_solution(9486343873522222713)
XLA Ops:
  0.6 34.6 %shard_map.94 = (bf16[1,128,8192]{2,1,0:T(8,128)(2,1)S(1)}, bf16[1,128,1024]{2,1,0:T(8,128)(2,1)S(1)}, bf16[1,128,1024]{2,1,0:T(8,128)(2,1)S(1)}) custom-call(bf16[1,128,8192]{2,1,0:T(8,128)(2,1)} %q_hbm.1, bf16[1,128,1024]{2,1,0:T(8,128)(2,1)} %k_hbm.1, bf16[1,128,1024]{2,1,0:T(8,128)(2,1)} %v_hbm.1, bf16[1,128,8192]{2,1,0:T(8,128)(2,1)} %g_hbm.1, ...), custom_call_target="tpu_custom_call" | custom-call | tf_op jit(solution)/shard_map/pallas_call | solution.py:512
  35.2 1.5 %shard_map.95 = (bf16[1,128,8192]{2,1,0:T(8,128)(2,1)}, bf16[1,128,1024]{2,1,0:T(8,128)(2,1)}, bf16[1,128,1024]{2,1,0:T(8,128)(2,1)}) custom-call(bf16[1,128,8192]{2,1,0:T(8,128)(2,1)S(1)} %get-tuple-element.6.held_q, bf16[1,128,1024]{2,1,0:T(8,128)(2,1)S(1)} %get-tuple-element.7.held_k, bf16[1,128,1024]{2,1,0:T(8,128)(2,1)S(1)} %get-tuple-element.8.held_v), custom_call_target="tpu_custom_call" | custom-call | tf_op jit(solution)/shard_map/pallas_call | solution.py:562
